TPU v7x, 512 devices: a whole 4x8x8 slice. The times are simulated.
512 devices in a mesh: seq: 64 (over y, z), tp: 8 (over x, core).
Axes of the slice: x: 4, y: 8, z: 8, core: 2. Of those that a mesh axis runs over, the one named last changes fastest.
Arguments:
- queries: bfloat16 [16384, 8192], P('seq', 'tp'), may hold values from -12 to 12
- kv_rows: bfloat16 [16384, 2048], P('seq', 'tp'), may hold values from -6 to 6
- vertical: int32 [64, 32], replicated, may hold values from 0 to 255, as said below
- slash: int32 [64, 8], replicated, may hold values from 0 to 11, as said below
Outputs:
- attended: bfloat16 [16384, 8192], P(('seq', 'tp'))
Inputs may be any that keep to these rules, and one draw needn't show every extreme that they name: `vertical`: each row lists 32 distinct blocks in rising order and includes block 0 and block 255. The heads that share one key-value head list together exactly 48 distinct blocks. `slash`: each row lists 8 distinct offsets in rising order, the first 0 and the last 11.
All inputs are finite; a program needn't handle non-finite values.
Results may differ from a plain program's by a relative error of at most 0.0045.
Values may be sent and summed in bfloat16 or wider, within the bound.
A program may use at most 64 MiB of HBM per device.

v0:
```python
import jax
import jax.numpy as jnp
from jax import lax
from jax.sharding import PartitionSpec as P

HEAD_SIZE = 128
BLK = 64


def as_sent(array):

    def short(part):
        return part.astype(jnp.bfloat16) if part.dtype == jnp.float32 else part

    return jax.tree.map(short, array)


def key_mask(bids, vertical_row, srow):
    dist = bids[:, None] - vertical_row[None, :]
    hit = jnp.any(dist[:, :, None] == srow[None, None, :], axis=2)
    live_v = jnp.logical_and(dist >= 0, jnp.logical_not(hit))
    live_s = bids[:, None] - srow[None, :] >= 0
    live = jnp.concatenate([live_v, live_s], axis=1)
    diag = jnp.concatenate([jnp.zeros(vertical_row.shape, bool), srow == 0])
    rows = jnp.arange(BLK, dtype=jnp.int32)
    lower = rows[None, :] <= rows[:, None]
    return live[:, None, :, None] & (
        jnp.logical_not(diag)[None, None, :, None] | lower[None, :, None, :]
    )


def attend(query_block, vert_block, slash_block, bids, vertical_row, srow):
    count_v = vert_block.shape[0]
    scale = 1.0 / HEAD_SIZE**0.5
    logit_vert = jnp.einsum(
        "unz,syz->unsy",
        query_block,
        vert_block[..., :HEAD_SIZE],
        preferred_element_type=jnp.float32,
    )
    logit_slash = jnp.einsum(
        "unz,suyz->unsy",
        query_block,
        slash_block[..., :HEAD_SIZE],
        preferred_element_type=jnp.float32,
    )
    logit_matrix = jnp.concatenate([logit_vert, logit_slash], axis=2) * scale
    mask = key_mask(bids, vertical_row, srow)
    logit_matrix = jnp.where(mask, logit_matrix, -1e30)
    top = jnp.max(logit_matrix, axis=(2, 3), keepdims=True)
    weights = jnp.where(mask, jnp.exp(logit_matrix - top), 0.0)
    total = jnp.sum(weights, axis=(2, 3))
    probabilities = weights.astype(jnp.bfloat16)
    weighted_sum = jnp.einsum(
        "unsy,syd->und",
        probabilities[:, :, :count_v],
        vert_block[..., HEAD_SIZE:],
        preferred_element_type=jnp.float32,
    )
    weighted_sum = weighted_sum + jnp.einsum(
        "unsy,suyd->und",
        probabilities[:, :, count_v:],
        slash_block[..., HEAD_SIZE:],
        preferred_element_type=jnp.float32,
    )
    return (weighted_sum / total[..., None]).astype(jnp.bfloat16)


def slash_slices(table, starts, key_value_head, block_list):
    pieces = []
    for index in range(starts.shape[0]):
        piece = lax.dynamic_slice(
            table,
            (starts[index], 0, key_value_head, 0),
            (block_list, table.shape[1], 1, table.shape[3]),
        )
        pieces.append(piece[:, :, 0])
    return jnp.stack(pieces, axis=0)


def per_device(queries, kv_rows, vertical, slash):
    tok = queries.shape[0]
    n_tp = lax.axis_size("tp")
    heads_loc = vertical.shape[0] // n_tp
    kv_loc = kv_rows.shape[1] // (2 * HEAD_SIZE)
    group = heads_loc // kv_loc
    block_list = tok // BLK
    seq_pos = lax.axis_index("seq")
    tp_pos = lax.axis_index("tp")
    my_vert = lax.dynamic_slice_in_dim(vertical, tp_pos * heads_loc, heads_loc, 0)
    my_slash = lax.dynamic_slice_in_dim(slash, tp_pos * heads_loc, heads_loc, 0)
    first = seq_pos * block_list
    bids = first + jnp.arange(block_list, dtype=jnp.int32)
    full = lax.all_gather(kv_rows, "seq", axis=0, tiled=True)
    index_table = full.reshape(full.shape[0] // BLK, BLK, kv_loc, 2 * HEAD_SIZE)
    front = 3 * block_list
    padded = jnp.concatenate(
        [jnp.zeros((front, BLK, kv_loc, 2 * HEAD_SIZE), index_table.dtype), index_table], axis=0
    )

    def gather_rows(key_value_head, vertical_row, srow):
        vert_block = index_table[vertical_row, :, key_value_head]
        starts = first + front - srow
        return (vert_block, slash_slices(padded, starts, key_value_head, block_list))

    qheads = jnp.transpose(queries.reshape(block_list, BLK, heads_loc, HEAD_SIZE), (2, 0, 1, 3))

    def one_head(item):
        query_block, vertical_row, srow, key_value_head = item
        vert_block, slash_block = gather_rows(key_value_head, vertical_row, srow)
        return attend(query_block, vert_block, slash_block, bids, vertical_row, srow)

    owners = jnp.arange(heads_loc, dtype=jnp.int32) // group
    outputs = lax.map(one_head, (qheads, my_vert, my_slash, owners))
    attn = jnp.transpose(outputs, (1, 2, 0, 3)).reshape(tok, heads_loc * HEAD_SIZE)
    return lax.all_to_all(as_sent(attn), "tp", split_axis=0, concat_axis=1, tiled=True).astype(
        attn.dtype
    )


def solution(mesh):
    return jax.shard_map(
        per_device,
        mesh=mesh,
        in_specs=(P("seq", "tp"), P("seq", "tp"), P(), P()),
        out_specs=P(("seq", "tp"), None),
        check_vma=False,
    )
```

profile of v0, /device:TPU:1, one launch (start us, length us, event | category | flops | bytes accessed | tf_op | source)
XLA Modules:
  0.0 460.2 jit_solution(17042066455035108971)
XLA Ops:
  10.4 104.9 %all-gather.2.cloned.1.call-done = bf16[16384,256]{1,0:T(8,128)(2,1)} async-done(((bf16[256,256]{1,0:T(8,128)(2,1)}), bf16[16384,256]{1,0:T(8,128)(2,1)}) %all-gather.2.cloned.1.call-update) | async-done | bytes 8388624 | tf_op jit(solution)/shard_map/all_gather | solution.py:94
  115.2 8.4 %concatenate.19 = bf16[268,64,1,256]{3,1,0,2:T(8,128)(2,1)} pad(bf16[256,64,1,256]{3,1,0,2:T(8,128)(2,1)} %bitcast.144, bf16[]{:T(256)} %constant.98.clone.1), padding=12_0x0_0x0_0x0_0 | pad | bytes 17170434 | tf_op jit(solution)/shard_map/concatenate | solution.py:97
  123.7 313.1 %while.13 = (s32[]{:T(128)}, bf16[8,4,64,128]{3,2,1,0:T(8,128)(2,1)}, s32[8,32]{1,0:T(8,128)S(1)}, s32[8,8]{1,0:T(8,128)S(1)}, bf16[8,4,64,128]{3,2,1,0:T(8,128)...) while((s32[]{:T(128)}, ...), condition=%wide.region_4.5_spmd.clone, body=%wide.region_0.4_spmd.clone.sunk | while | flops 344332768 | bytes 21678552 | solution.py:114
  150.7 4.0 gather_fusion
  154.7 1.6 fusion.53
  156.6 1.4 fusion.55
  158.1 3.0 fusion.56
  189.9 4.0 gather_fusion
  193.9 1.6 fusion.53
  195.8 1.4 fusion.55
  197.2 3.0 fusion.56
  229.0 4.0 gather_fusion
  233.0 1.6 fusion.53
  234.9 1.4 fusion.55
  236.3 3.0 fusion.56
  268.1 4.0 gather_fusion
  272.1 1.6 fusion.53
  274.0 1.4 fusion.55
  275.5 3.0 fusion.56
  307.3 4.0 gather_fusion
  311.3 1.6 fusion.53
  314.6 3.0 fusion.56
  346.4 4.0 gather_fusion
  350.4 1.6 fusion.53
  353.7 3.0 fusion.56
  385.5 4.0 gather_fusion
  389.6 1.6 fusion.53
  392.9 3.0 fusion.56
  424.7 4.0 gather_fusion
  428.7 1.6 fusion.53
  432.0 3.0 fusion.56
  438.4 14.1 %all_to_all.19 = bf16[8,32,1024]{2,1,0:T(8,128)(2,1)S(1)} all-to-all(bf16[8,32,1024]{2,1,0:T(8,128)(2,1)S(1)} %all_to_all.14), channel_id=1, replica_groups=mesh['seq'=64,'tp'=8] {'tp'}, dimensions={0} | all-to-all | bytes 1048576 | tf_op jit(solution)/shard_map/all_to_all | solution.py:116
  (228 shorter events, 109.5 us)
Async XLA Ops:
  6.5 0.7 copy-start
  6.5 108.7 %all-gather.2.cloned.1.call-start = ((), (), s32[]{:S(2)}) async-start(), calls=%async_computation.1 | async-start | bytes 8519680 | tf_op jit(solution)/shard_map/all_gather | solution.py:94
Sparse Core Ops, SparseCore 0:
  10.4 104.8 all-gather.1
where the time goes:
time: 465 us; the launch traced here: 460 us
  loops' own time  135 us (29%)
  local copies, waits for them, and re-layouts  115 us (25%)
  waiting for transfers between devices  106 us (23%)
  other arithmetic  41.5 us (9%)
  matrix products  35.1 us (8%)
  blocking collectives  14.1 us (3%)
  between operations  13.4 us (3%)
    another operation x1, loops' own time, per_device(): outputs = lax.map(one_head, (qheads, my_vert, my_slash, owners))  135 us
    all_gather x1, waiting for transfers between devices, per_device(): full = lax.all_gather(kv_rows, 'seq', axis=0, tiled=True)  105 us
    while x56, local copies, waits for them, and re-layouts  51.4 us
    gather x8, local copies, waits for them, and re-layouts, gather_rows(): vert_block = index_table[vertical_row, :, key_value_head]  32 us
    reduce_sum x8, other arithmetic, attend(): total = jnp.sum(weights, axis=(2, 3))  24.2 us
    all_to_all x1, blocking collectives, per_device(): lax.all_to_all(as_sent(attn), 'tp', split_axis=0, concat_axis=1, tiled=True)  14.1 us
    dot_general x8, matrix products, attend(): jnp.einsum('unz,syz->unsy', query_block, vert_block[..., :HEAD_SIZE], pre...  12.5 us
    reduce_max x8, other arithmetic, attend(): top = jnp.max(logit_matrix, axis=(2, 3), keepdims=True)  11.5 us
  transfers between devices with their start and end apart: 1, of which 1 were waited for; matrix products, arithmetic and copies ran while one was open for 1% of the time, Pallas kernels for 0%

commit v1 on v0

--- a/solution.py
+++ b/solution.py
@@ -91,7 +91,9 @@
     my_slash = lax.dynamic_slice_in_dim(slash, tp_pos * heads_loc, heads_loc, 0)
     first = seq_pos * block_list
     bids = first + jnp.arange(block_list, dtype=jnp.int32)
-    full = lax.all_gather(kv_rows, "seq", axis=0, tiled=True)
+    full = jnp.concatenate(
+        lax.all_to_all(jnp.stack([kv_rows] * lax.axis_size("seq")), "seq", 0, 0), axis=0
+    )
     index_table = full.reshape(full.shape[0] // BLK, BLK, kv_loc, 2 * HEAD_SIZE)
     front = 3 * block_list
     padded = jnp.concatenate(

time: 465 us -> 641 us (1.38)
  the two profiles are of different devices: /device:TPU:1 before, /device:TPU:216 now
where the time goes in v1:
time: 641 us; the launch traced here: 637 us
  waiting for transfers between devices  278 us (43%)
  loops' own time  135 us (21%)
  local copies, waits for them, and re-layouts  119 us (19%)
  other arithmetic  41.5 us (6%)
  matrix products  35.1 us (5%)
  blocking collectives  14.5 us (2%)
  starting transfers between devices  14 us (2%)
    all_to_all x1, waiting for transfers between devices, per_device(): lax.all_to_all(jnp.stack([kv_rows] * lax.axis_size('seq')), 'seq', 0, 0)  278 us
    another operation x1, loops' own time, per_device(): outputs = lax.map(one_head, (qheads, my_vert, my_slash, owners))  135 us
    while x56, local copies, waits for them, and re-layouts  51.4 us
    gather x8, local copies, waits for them, and re-layouts, gather_rows(): vert_block = index_table[vertical_row, :, key_value_head]  32 us
    reduce_sum x8, other arithmetic, attend(): total = jnp.sum(weights, axis=(2, 3))  24.2 us
    all_to_all x1, blocking collectives, per_device(): lax.all_to_all(as_sent(attn), 'tp', split_axis=0, concat_axis=1, tiled=True)  14.5 us
    all_to_all x1, starting transfers between devices, per_device(): lax.all_to_all(jnp.stack([kv_rows] * lax.axis_size('seq')), 'seq', 0, 0)  14 us
  transfers between devices with their start and end apart: 1, of which 1 were waited for; matrix products, arithmetic and copies ran while one was open for 0% of the time, Pallas kernels for 0%

profile of v1, /device:TPU:216, one launch (start us, length us, event | category | flops | bytes accessed | tf_op | source)
XLA Modules:
  0.0 636.7 jit_solution(8181299796096214101)
XLA Ops:
  0.0 5.1 stack.6
  5.2 14.0 %all-to-all-start = ((bf16[64,256,256]{2,1,0:T(8,128)(2,1)}), bf16[64,256,256]{2,1,0:T(8,128)(2,1)}, u32[]{:S(2)}, u32[]{:S(2)}) async-start(bf16[64,256,256]{2,1,0:T(8,128)(2,1)} %stack.6), calls=%async_computation | async-start | bytes 16777216 | tf_op jit(solution)/shard_map/all_to_all | solution.py:95
  20.6 277.5 %all-to-all-done = bf16[64,256,256]{2,1,0:T(8,128)(2,1)} async-done(((bf16[64,256,256]{2,1,0:T(8,128)(2,1)}), bf16[64,256,256]{2,1,0:T(8,128)(2,1)}, u32[]{:S(2)}, u32[]{:S(2)}) %all-to-all-start) | async-done | bytes 8388640 | tf_op jit(solution)/shard_map/all_to_all | solution.py:95
  298.1 8.4 %concatenate.19 = bf16[268,64,1,256]{3,1,0,2:T(8,128)(2,1)} pad(bf16[256,64,1,256]{3,1,0,2:T(8,128)(2,1)} %bitcast.1, bf16[]{:T(256)} %constant.98.clone.1), padding=12_0x0_0x0_0x0_0 | pad | bytes 17170434 | tf_op jit(solution)/shard_map/concatenate | solution.py:99
  306.6 313.2 %while.13 = (s32[]{:T(128)}, bf16[8,4,64,128]{3,2,1,0:T(8,128)(2,1)}, s32[8,32]{1,0:T(8,128)S(1)}, s32[8,8]{1,0:T(8,128)S(1)}, bf16[8,4,64,128]{3,2,1,0:T(8,128)...) while((s32[]{:T(128)}, ...), condition=%wide.region_4.5_spmd.clone, body=%wide.region_0.4_spmd.clone.sunk | while | flops 344332768 | bytes 21678552 | solution.py:116
  333.6 4.0 gather_fusion
  337.6 1.6 fusion.53
  339.5 1.4 fusion.55
  341.0 3.0 fusion.56
  372.8 4.0 gather_fusion
  376.8 1.6 fusion.53
  380.1 3.0 fusion.56
  412.0 4.0 gather_fusion
  416.0 1.6 fusion.53
  419.3 3.0 fusion.56
  451.1 4.0 gather_fusion
  455.1 1.6 fusion.53
  457.0 1.4 fusion.55
  458.4 3.0 fusion.56
  490.3 4.0 gather_fusion
  494.3 1.6 fusion.53
  497.6 3.0 fusion.56
  529.4 4.0 gather_fusion
  533.4 1.6 fusion.53
  536.8 3.0 fusion.56
  568.6 4.0 gather_fusion
  572.6 1.6 fusion.53
  575.9 3.0 fusion.56
  607.7 4.0 gather_fusion
  611.7 1.6 fusion.53
  615.1 3.0 fusion.56
  621.4 14.5 %all_to_all.24 = bf16[8,32,1024]{2,1,0:T(8,128)(2,1)S(1)} all-to-all(bf16[8,32,1024]{2,1,0:T(8,128)(2,1)S(1)} %all_to_all.18), channel_id=1, replica_groups=mesh['seq'=64,'tp'=8] {'tp'}, dimensions={0} | all-to-all | bytes 1048576 | tf_op jit(solution)/shard_map/all_to_all | solution.py:118
  (232 shorter events, 110.4 us)
Async XLA Ops:
  0.0 19.2 %copy-start = (s32[64,32]{0,1:T(8,128)S(1)}, s32[64,32]{0,1:T(8,128)}, u32[]{:S(2)}) copy-start(s32[64,32]{0,1:T(8,128)} %param.8) | copy-start | bytes 24580
  5.1 14.2 %copy-start.2 = (s32[64,8]{0,1:T(8,128)S(1)}, s32[64,8]{0,1:T(8,128)}, u32[]{:S(2)}) copy-start(s32[64,8]{0,1:T(8,128)} %param.9) | copy-start | bytes 6148
  5.2 14.3 %copy-start.1 = (bf16[256,1024]{1,0:T(8,128)(2,1)S(1)}, bf16[256,1024]{1,0:T(8,128)(2,1)}, u32[]{:S(2)}) copy-start(bf16[256,1024]{1,0:T(8,128)(2,1)} %param.6) | copy-start | bytes 1572868
  5.2 293.0 %all-to-all-start = ((bf16[64,256,256]{2,1,0:T(8,128)(2,1)}), bf16[64,256,256]{2,1,0:T(8,128)(2,1)}, u32[]{:S(2)}, u32[]{:S(2)}) async-start(bf16[64,256,256]{2,1,0:T(8,128)(2,1)} %stack.6), calls=%async_computation | async-start | bytes 16777216 | tf_op jit(solution)/shard_map/all_to_all | solution.py:95
